TPU v7x, 32 devices: a whole 2x2x4 slice. The times are simulated.
32 devices in a mesh: groups: 2 (over x), fsdp: 16 (over z, y, core).
Axes of the slice: x: 2, y: 2, z: 4, core: 2. Of those that a mesh axis runs over, the one named last changes fastest.
Arguments:
- obs_feat: bfloat16 [12288, 2048], P(('groups', 'fsdp')), parts along dimension 0, may hold values from -6 to 6
- reward: float32 [512, 24], P(('groups', 'fsdp')), parts along dimension 0, may hold values from -22 to 22
- value_old: float32 [512, 25], P(('groups', 'fsdp')), parts along dimension 0, may hold values from -6 to 6
- done: int32 [512, 24], P(('groups', 'fsdp')), parts along dimension 0, may hold values 0 or 1
- minibatch_perm: int32 [12288], P(('groups', 'fsdp')), parts along dimension 0, may hold values from 0 to 6143, as said below
- old_mean: bfloat16 [12288, 12], P(('groups', 'fsdp')), parts along dimension 0, may hold values from -6 to 6
- noise: bfloat16 [12288, 12], P(('groups', 'fsdp')), parts along dimension 0, may hold values from -6 to 6
- gain_in: float32 [2048], replicated, may hold values from 0.5 to 1.5
- out_weight: bfloat16 [2048, 2048], P('fsdp'), may hold values from -0.125 to 0.125
- head_weight: bfloat16 [2048, 13], replicated, may hold values from -0.125 to 0.125
- log_std: float32 [12], replicated, may hold values from 0.7 to 1.3
Outputs:
- hidden_out: bfloat16 [12288, 2048], P(('groups', 'fsdp')), parts along dimension 0
- grad_weight: float32 [4096, 2048], P(('groups', 'fsdp')), parts along dimension 0
- grad_head: float32 [4096, 13], P('groups'), parts along dimension 0
- grad_std: float32 [24], P('groups'), parts along dimension 0
There are 2 independent parts, one for each index of `groups`. A program takes and returns all parts, laid end to end along the dimension named above; an argument that names none is the same for every part. Nothing has to cross between parts.
Inputs may be any that keep to these rules, and one draw needn't show every extreme that they name: `minibatch_perm`: rows of one index of fsdp go 24 to each index of fsdp; the block of 384 minibatch positions of index j holds at positions j * 384 + s * 24 + c the rows from index s; a permutation of all rows.
All inputs are finite; a program needn't handle non-finite values. No bound on the sum of `done` on one device may be relied on, other than what follows from the above.
Results may differ from a plain program's by a relative error of at most 0.0095.
Values may be sent and summed in bfloat16 or wider, within the bound.
A program may use at most 128 MiB of HBM per device.

v0:
```python
import jax
import jax.numpy as jnp
from jax import lax
from jax.sharding import PartitionSpec as P

GAMMA = 0.99
LAMBDA_GAE = 0.95
CLIP_EPS = 0.2
NORM_EPS = 1e-05


def advantages(reward, value_old, done):
    keep = 1.0 - done.astype(jnp.float32)
    deltas = reward + GAMMA * value_old[:, 1:] * keep - value_old[:, :-1]

    def walk(carry, inputs):
        dstep, kstep = inputs
        carry = dstep + GAMMA * LAMBDA_GAE * kstep * carry
        return (carry, carry)

    start = jnp.zeros((reward.shape[0],), jnp.float32)
    _, stacked = lax.scan(walk, start, (deltas.T, keep.T), reverse=True)
    gae = stacked.T
    return (gae.reshape(-1), (gae + value_old[:, :-1]).reshape(-1))


def compute_rows(
    rows_x, old_mean, noise, adv_b, ret_b, gain_in, out_weight, head_weight, log_std, scale
):
    xf = rows_x.astype(jnp.float32)
    normed = (xf * lax.rsqrt(jnp.mean(xf * xf, -1, keepdims=True) + NORM_EPS) * gain_in).astype(
        jnp.bfloat16
    )
    columns = normed
    hidden = xf + jnp.dot(
        columns,
        lax.all_gather(out_weight, "fsdp", axis=0, tiled=True),
        preferred_element_type=jnp.float32,
    )
    rinv = lax.rsqrt(jnp.mean(hidden * hidden, -1, keepdims=True) + NORM_EPS)
    hnorm = hidden * rinv
    hnorm_b = hnorm.astype(jnp.bfloat16)
    heads = jnp.dot(hnorm_b, head_weight, preferred_element_type=jnp.float32)
    nact = log_std.shape[0]
    mean_act = heads[:, :nact]
    value = heads[:, nact]
    std_dev = jnp.exp(log_std)
    offset = old_mean.astype(jnp.float32) - mean_act
    sample = noise.astype(jnp.float32)
    logr = jnp.sum(-sample * offset / std_dev - offset * offset / (2.0 * std_dev * std_dev), -1)
    ratio = jnp.exp(logr)
    advant = adv_b.astype(jnp.float32)
    clipped = jnp.clip(ratio, 1.0 - CLIP_EPS, 1.0 + CLIP_EPS)
    active = ratio * advant <= clipped * advant
    gratio = jnp.where(active, -scale * advant, 0.0)
    glogr = gratio * ratio
    gmean = glogr[:, None] * (sample / std_dev + offset / (std_dev * std_dev))
    gvalue = scale * (value - ret_b.astype(jnp.float32))
    std_local = jnp.sum(
        glogr[:, None] * (sample * offset / std_dev + offset * offset / (std_dev * std_dev)), 0
    )
    ghead = jnp.concatenate([gmean, gvalue[:, None]], 1)
    head_local = jnp.dot(hnorm_b.astype(jnp.float32).T, ghead, precision=lax.Precision.HIGHEST)
    ghn = jnp.dot(ghead, head_weight.astype(jnp.float32).T, precision=lax.Precision.HIGHEST)
    ghid = rinv * (ghn - hnorm * jnp.mean(ghn * hnorm, -1, keepdims=True))
    ghid_b = ghid.astype(jnp.bfloat16)
    columns = normed
    grad_weight = lax.psum_scatter(
        lax.dot_general(
            columns, ghid_b, (((0,), (0,)), ((), ())), preferred_element_type=jnp.float32
        ),
        "fsdp",
        scatter_dimension=0,
        tiled=True,
    )
    grad_head, grad_std = lax.psum((head_local, std_local), "fsdp")
    return (hidden.astype(jnp.bfloat16), grad_weight, grad_head, grad_std)


def local(
    obs_feat,
    reward,
    value_old,
    done,
    minibatch_perm,
    old_mean,
    noise,
    gain_in,
    out_weight,
    head_weight,
    log_std,
):
    gae, returns = advantages(reward, value_old, done)
    local_rows = obs_feat.shape[0]
    devices = lax.axis_size("fsdp")
    total_rows = local_rows * devices
    sums, squares = lax.psum((jnp.sum(gae), jnp.sum(gae * gae)), "fsdp")
    mean_adv = sums / total_rows
    var_adv = squares / total_rows - mean_adv * mean_adv
    adv_b = ((gae - mean_adv) * lax.rsqrt(var_adv + NORM_EPS)).astype(jnp.bfloat16)
    ret_b = returns.astype(jnp.bfloat16)
    scale = 1.0 / jnp.sqrt(jnp.float32(total_rows))
    per_peer = local_rows // devices
    send_slot = minibatch_perm // local_rows * per_peer + minibatch_perm % per_peer
    hidden_local, grad_weight, grad_head, grad_std = compute_rows(
        obs_feat, old_mean, noise, adv_b, ret_b, gain_in, out_weight, head_weight, log_std, scale
    )
    send_hidden = jnp.zeros_like(hidden_local).at[send_slot].set(hidden_local)
    hidden_out = lax.all_to_all(send_hidden, "fsdp", split_axis=0, concat_axis=0, tiled=True)
    return (hidden_out, grad_weight, grad_head, grad_std)


def solution(mesh):
    return jax.shard_map(
        local,
        mesh=mesh,
        in_specs=(
            P(("groups", "fsdp"), None),
            P(("groups", "fsdp"), None),
            P(("groups", "fsdp"), None),
            P(("groups", "fsdp"), None),
            P(("groups", "fsdp")),
            P(("groups", "fsdp"), None),
            P(("groups", "fsdp"), None),
            P(),
            P("fsdp", None),
            P(),
            P(),
        ),
        out_specs=(
            P(("groups", "fsdp"), None),
            P(("groups", "fsdp"), None),
            P("groups", None),
            P("groups"),
        ),
        check_vma=False,
    )
```

profile of v0, /device:TPU:0, one launch (start us, length us, event | category | flops | bytes accessed | tf_op | source)
XLA Modules:
  0.0 389.4 jit_solution(8685224248298809231)
XLA Ops:
  7.2 0.0 copy-start
  7.2 0.0 all-gather.2.cloned.1.call-start
  7.2 0.7 all-gather.2.cloned.1.call-update
  7.9 0.0 all-reduce.3.cloned.1.call-start
  8.0 0.9 fusion.31
  8.8 0.1 copy.26
  8.9 0.1 copy.27
  9.0 1.8 while.17
  10.8 0.1 copy.28
  10.8 0.6 fusion.29
  11.5 0.6 reduce_sum.66
  12.1 36.7 %all-reduce = (f32[]{:T(128)}, f32[]{:T(128)}) all-reduce(f32[]{:T(128)} %fusion.29, f32[]{:T(128)} %reduce_sum.66), channel_id=1, replica_groups=mesh['groups'=2,'fsdp'=16] {'fsdp'}, use_global_device_ids=true, to_apply=%region_9.10 | all-reduce | flops 2 | bytes 16 | tf_op jit(solution)/shard_map/psum | solution.py:97
  51.4 0.7 fusion.33
  52.1 0.1 reshape.79
  52.2 0.1 reshape.80
  52.3 1.8 fusion.2
  54.1 0.7 fusion.39
  54.8 32.7 %all-gather.2.cloned.1.call-done = bf16[2048,2048]{1,0:T(8,128)(2,1)} async-done(((bf16[128,2048]{1,0:T(8,128)(2,1)}), bf16[2048,2048]{1,0:T(8,128)(2,1)}) %all-gather.2.cloned.1.call-update) | async-done | bytes 8388624 | tf_op jit(solution)/shard_map/all_gather | solution.py:37
  87.5 7.9 %multiply_reduce_fusion.1 = (f32[384]{0:T(512)S(1)}, f32[384,2048]{1,0:T(8,128)S(1)}) fusion(bf16[2048,2048]{1,0:T(8,128)(2,1)} %all-gather.2.cloned.1.call-done, bf16[384,2048]{1,0:T(8,128)(2,1)} %param.13, f32[2048]{0:T(1024)} %param.20, f32[384]{0:T(512)S(1)} %add_rsqrt_fusion.1), kind=kOutput, calls=%fused_computation.12 | convolution fusion | flops 3227516416 | bytes 13118464 | tf_op jit(solution)/shard_map/dot_general | solution.py:35
  95.3 0.0 copy-start.2
  95.3 0.0 copy-start.3
  95.4 0.2 multiply_convert_fusion.1
  95.6 0.0 copy-done
  95.6 0.5 fusion.40
  96.1 0.0 copy-done.2
  96.1 0.0 copy-done.3
  96.2 0.1 fusion.23
  96.3 0.2 fusion.24
  96.5 0.0 copy-start.4
  96.5 3.4 multiply_reduce_fusion
  99.8 1.4 fusion.25
  101.2 0.0 all-reduce.3.cloned.1.call-update
  101.3 0.2 reduce-scatter.2.cloned.1.call-start
  101.5 0.0 copy-done.4
  101.5 12.9 %fusion.5 = f32[2048,2048]{1,0:T(8,128)} fusion(f32[384,2048]{1,0:T(8,128)} %get-tuple-element.155, f32[384,2048]{1,0:T(8,128)S(1)} %get-tuple-element.153, f32[384]{0:T(512)S(1)} %broadcast_multiply_fusion, f32[384]{0:T(512)S(1)} %add_rsqrt_fusion, bf16[384,2048]{1,0:T(8,128)(2,1)} %param.13, f32[2048]{0:T(1024)S(1)} %copy-done.4, f32[384]{0:T(512)S(1)} %add_rsqrt_fusion.1), kind=kOutput, calls=%fused_computation.14 | convolution fusion | flops 3228303360 | bytes 24654336 | tf_op jit(solution)/shard_map/dot_general | solution.py:69
  114.4 0.0 copy-start.5
  114.4 0.0 reduce-scatter.2.cloned.1.call-update
  114.4 0.7 copy-done.5
  115.1 4.1 %scatter_custom_fusion = bf16[384,2048]{1,0:T(8,128)(2,1)} fusion(s32[384]{0:T(512)S(1)} %compare_select_fusion, f32[384,2048]{1,0:T(8,128)S(1)} %get-tuple-element.153, bf16[]{:T(256)} %constant.88.clone.1), kind=kCustom, calls=%fused_computation.17 | custom fusion | flops 786432 | bytes 4718594 | tf_op jit(solution)/shard_map/scatter | solution.py:108
  119.2 3.7 all-to-all-start
  122.9 54.6 %psum.31 = f32[12]{0:T(128)} all-reduce(f32[12]{0:T(128)S(1)} %get-tuple-element.143), channel_id=1, replica_groups=mesh['groups'=2,'fsdp'=16] {'fsdp'}, use_global_device_ids=true, to_apply=%region_14.15 | all-reduce | flops 12 | bytes 96 | tf_op jit(solution)/shard_map/psum | solution.py:76
  177.5 0.0 all-to-all-done
  177.5 20.0 %all-reduce.3.cloned.1.call-done = f32[2048,13]{0,1:T(8,128)} async-done(((f32[2048,13]{0,1:T(8,128)}), f32[2048,13]{0,1:T(8,128)}) %all-reduce.3.cloned.1.call-update) | async-done | bytes 106512 | tf_op jit(solution)/shard_map/psum | solution.py:76
  197.5 0.0 copy-start.1
  197.5 183.6 %reduce-scatter.2.cloned.1.call-done = f32[128,2048]{1,0:T(8,128)} async-done(((f32[2048,2048]{1,0:T(8,128)}), f32[128,2048]{1,0:T(8,128)}) %reduce-scatter.2.cloned.1.call-update) | async-done | bytes 1048592 | tf_op jit(solution)/shard_map/reduce_scatter | solution.py:68
  381.1 1.1 copy.41
  382.2 0.0 copy-done.1
  382.2 0.7 copy.42
  (56 shorter events, 1.5 us)
Async XLA Ops:
  7.2 88.4 %copy-start = (bf16[2048,13]{0,1:T(8,128)(2,1)S(1)}, bf16[2048,13]{0,1:T(8,128)(2,1)}, u32[]{:S(2)}) copy-start(bf16[2048,13]{0,1:T(8,128)(2,1)} %param.22) | copy-start | bytes 159748
  7.2 80.3 %all-gather.2.cloned.1.call-start = ((), (), s32[]{:S(2)}) async-start(), calls=%async_computation.2 | async-start | bytes 8912896 | tf_op jit(solution)/shard_map/all_gather | solution.py:37
  7.9 189.6 %all-reduce.3.cloned.1.call-start = ((), (), s32[]{:S(2)}) async-start(), calls=%async_computation.4 | async-start | bytes 262144 | tf_op jit(solution)/shard_map/psum | solution.py:76
  95.3 0.8 copy-start.2
  95.3 0.8 copy-start.3
  96.5 5.0 %copy-start.4 = (f32[2048]{0:T(1024)S(1)}, f32[2048]{0:T(1024)}, u32[]{:S(2)}) copy-start(f32[2048]{0:T(1024)} %param.20) | copy-start | bytes 24580
  101.3 279.8 %reduce-scatter.2.cloned.1.call-start = ((), (), s32[]{:S(2)}) async-start(), calls=%async_computation.3 | async-start | bytes 17825792 | tf_op jit(solution)/shard_map/reduce_scatter | solution.py:68
  114.4 0.7 copy-start.5
  119.2 58.3 %all-to-all-start = ((bf16[16,24,2048]{2,1,0:T(8,128)(2,1)}), bf16[16,24,2048]{2,1,0:T(8,128)(2,1)S(1)}, u32[]{:S(2)}, u32[]{:S(2)}) async-start(bf16[16,24,2048]{2,1,0:T(8,128)(2,1)} %bitcast.39), calls=%async_computation | async-start | bytes 3145728 | tf_op jit(solution)/shard_map/all_to_all | solution.py:109
  197.5 184.8 %copy-start.1 = (f32[2048,13]{0,1:T(8,128)S(1)}, f32[2048,13]{0,1:T(8,128)}, u32[]{:S(2)}) copy-start(f32[2048,13]{0,1:T(8,128)} %all-reduce.3.cloned.1.call-done) | copy-start | bytes 319492
Sparse Core Ops, SparseCore 0:
  10.2 77.2 all-gather.1
  101.4 96.0 all-reduce.2
  202.2 178.8 reduce-scatter.1
where the time goes:
time: 390 us; the launch traced here: 389 us
  waiting for transfers between devices  237 us (61%)
  blocking collectives  91.3 us (23%)
  matrix products  26 us (7%)
  between operations  16.5 us (4%)
  other arithmetic  10.4 us (3%)
  starting transfers between devices  4.01 us (1%)
    reduce_scatter x1, waiting for transfers between devices, compute_rows(): lax.psum_scatter(lax.dot_general(columns, ghid_b, (((0,), (0,)), ((), ())...  184 us
    psum x1, blocking collectives, compute_rows(): grad_head, grad_std = lax.psum((head_local, std_local), 'fsdp')  54.6 us
    psum x1, blocking collectives, local(): sums, squares = lax.psum((jnp.sum(gae), jnp.sum(gae * gae)), 'fsdp')  36.7 us
    all_gather x1, waiting for transfers between devices, compute_rows(): lax.all_gather(out_weight, 'fsdp', axis=0, tiled=True)  32.7 us
    psum x1, waiting for transfers between devices, compute_rows(): grad_head, grad_std = lax.psum((head_local, std_local), 'fsdp')  20 us
    dot_general x1, matrix products, compute_rows(): lax.dot_general(columns, ghid_b, (((0,), (0,)), ((), ())), preferred_elem...  12.9 us
    dot_general x1, matrix products, compute_rows(): jnp.dot(columns, lax.all_gather(out_weight, 'fsdp', axis=0, tiled=True),...  7.85 us
  transfers between devices with their start and end apart: 4, of which 3 were waited for; matrix products, arithmetic and copies ran while one was open for 6% of the time, Pallas kernels for 0%

commit v1 on v0

--- a/solution.py
+++ b/solution.py
@@ -7,6 +7,19 @@
 LAMBDA_GAE = 0.95
 CLIP_EPS = 0.2
 NORM_EPS = 1e-05
+
+
+def gather_around(x, axis, dim):
+    ways = lax.axis_size(axis)
+    up = [(d, (d + 1) % ways) for d in range(ways)]
+    down = [(d, (d - 1) % ways) for d in range(ways)]
+    earlier, later = ([x], [x])
+    for _ in range(ways // 2):
+        earlier.append(lax.ppermute(earlier[-1], axis, up))
+    for _ in range((ways - 1) // 2):
+        later.append(lax.ppermute(later[-1], axis, down))
+    line = jnp.concatenate([*earlier[::-1], *later[1:]], axis=dim)
+    return jnp.roll(line, (lax.axis_index(axis) - ways // 2) * x.shape[dim], axis=dim)
 
 
 def advantages(reward, value_old, done):
@@ -33,9 +46,7 @@
     )
     columns = normed
     hidden = xf + jnp.dot(
-        columns,
-        lax.all_gather(out_weight, "fsdp", axis=0, tiled=True),
-        preferred_element_type=jnp.float32,
+        columns, gather_around(out_weight, "fsdp", 0), preferred_element_type=jnp.float32
     )
     rinv = lax.rsqrt(jnp.mean(hidden * hidden, -1, keepdims=True) + NORM_EPS)
     hnorm = hidden * rinv

time: 390 us -> 463 us (1.19)
  starting transfers between devices: 4.01 us -> 45.6 us
  local copies, waits for them, and re-layouts: 3.81 us -> 24 us
  waiting for transfers between devices: 237 us -> 256 us
    ppermute x0 -> x15, waiting for transfers between devices: none -> 47.4 us  [the longest x8 43.6 us: gather_around(): earlier.append(lax.ppermute(earlier[-1], axis, up))]
    ppermute x0 -> x15, starting transfers between devices: none -> 40.1 us  [the longest x8 22.7 us: gather_around(): earlier.append(lax.ppermute(earlier[-1], axis, up))]
    all_gather x1 -> x0, waiting for transfers between devices: 32.7 us -> none  [compute_rows(): lax.all_gather(out_weight, 'fsdp', axis=0, tiled=True)]
    unnamed x16 -> x53, local copies, waits for them, and re-layouts: 2.63 us -> 22.8 us
  transfers between devices with their start and end apart: 4 -> 18, of which waited for: 3 -> 10; matrix products, arithmetic and copies ran while one was open for 6% -> 8% of each run, Pallas kernels for 0% -> 0%
where the time goes in v1:
time: 463 us; the launch traced here: 462 us
  waiting for transfers between devices  256 us (55%)
  blocking collectives  87.3 us (19%)
  starting transfers between devices  45.6 us (10%)
  local copies, waits for them, and re-layouts  24 us (5%)
  matrix products  21.8 us (5%)
  between operations  17.1 us (4%)
  other arithmetic  10.5 us (2%)
    reduce_scatter x1, waiting for transfers between devices, compute_rows(): lax.psum_scatter(lax.dot_general(columns, ghid_b, (((0,), (0,)), ((), ())...  184 us
    psum x1, blocking collectives, compute_rows(): grad_head, grad_std = lax.psum((head_local, std_local), 'fsdp')  54.7 us
    ppermute x8, waiting for transfers between devices, gather_around(): earlier.append(lax.ppermute(earlier[-1], axis, up))  43.6 us
    psum x1, blocking collectives, local(): sums, squares = lax.psum((jnp.sum(gae), jnp.sum(gae * gae)), 'fsdp')  32.6 us
    psum x1, waiting for transfers between devices, compute_rows(): grad_head, grad_std = lax.psum((head_local, std_local), 'fsdp')  24.4 us
    unnamed x53, local copies, waits for them, and re-layouts  22.8 us
    ppermute x8, starting transfers between devices, gather_around(): earlier.append(lax.ppermute(earlier[-1], axis, up))  22.7 us
    ppermute x7, starting transfers between devices, gather_around(): later.append(lax.ppermute(later[-1], axis, down))  17.4 us
  transfers between devices with their start and end apart: 18, of which 10 were waited for; matrix products, arithmetic and copies ran while one was open for 8% of the time, Pallas kernels for 0%

profile of v1, /device:TPU:0, one launch (start us, length us, event | category | flops | bytes accessed | tf_op | source)
XLA Modules:
  0.0 462.1 jit_solution(7968159435080892518)
XLA Ops:
  7.2 0.5 collective-permute-start
  7.8 12.1 %collective-permute-done = bf16[128,2048]{1,0:T(8,128)(2,1)S(1)} collective-permute-done((bf16[128,2048]{1,0:T(8,128)(2,1)}, bf16[128,2048]{1,0:T(8,128)(2,1)S(1)}, u32[]{:S(2)}, u32[]{:S(2)}) %collective-permute-start) | collective-permute-done | bytes 524320 | tf_op jit(solution)/shard_map/ppermute | solution.py:18
  19.8 4.4 collective-permute-start.8
  24.3 7.0 %collective-permute-done.1 = bf16[128,2048]{1,0:T(8,128)(2,1)S(1)} collective-permute-done((bf16[128,2048]{1,0:T(8,128)(2,1)S(1)}, bf16[128,2048]{1,0:T(8,128)(2,1)S(1)}, u32[]{:S(2)}, u32[]{:S(2)}) %collective-permute-start.1) | collective-permute-done | bytes 524320 | tf_op jit(solution)/shard_map/ppermute | solution.py:18
  31.3 4.6 collective-permute-start.9
  35.9 6.8 %collective-permute-done.2 = bf16[128,2048]{1,0:T(8,128)(2,1)S(1)} collective-permute-done((bf16[128,2048]{1,0:T(8,128)(2,1)S(1)}, bf16[128,2048]{1,0:T(8,128)(2,1)S(1)}, u32[]{:S(2)}, u32[]{:S(2)}) %collective-permute-start.2) | collective-permute-done | bytes 524320 | tf_op jit(solution)/shard_map/ppermute | solution.py:18
  42.7 1.8 collective-permute-start.3
  44.4 2.9 collective-permute-start.10
  47.3 6.8 %collective-permute-done.3 = bf16[128,2048]{1,0:T(8,128)(2,1)S(1)} collective-permute-done((bf16[128,2048]{1,0:T(8,128)(2,1)S(1)}, bf16[128,2048]{1,0:T(8,128)(2,1)S(1)}, u32[]{:S(2)}, u32[]{:S(2)}) %collective-permute-start.3) | collective-permute-done | bytes 524320 | tf_op jit(solution)/shard_map/ppermute | solution.py:18
  54.1 3.8 collective-permute-start.4
  57.9 0.8 collective-permute-start.11
  58.7 6.9 %collective-permute-done.4 = bf16[128,2048]{1,0:T(8,128)(2,1)} collective-permute-done((bf16[128,2048]{1,0:T(8,128)(2,1)S(1)}, bf16[128,2048]{1,0:T(8,128)(2,1)}, u32[]{:S(2)}, u32[]{:S(2)}) %collective-permute-start.4) | collective-permute-done | bytes 524320 | tf_op jit(solution)/shard_map/ppermute | solution.py:18
  65.6 6.5 %collective-permute-start.5 = (bf16[128,2048]{1,0:T(8,128)(2,1)}, bf16[128,2048]{1,0:T(8,128)(2,1)}, u32[]{:S(2)}, u32[]{:S(2)}) collective-permute-start(bf16[128,2048]{1,0:T(8,128)(2,1)} %collective-permute-done.4), channel_id=1, source_target_pairs={{0,1},{1,2},{2,3},{3,4},{4,5},{5,6},{6,7},{7,8},{8,9},{9,10},{10,1... | collective-permute-start | bytes 1572872 | tf_op jit(solution)/shard_map/ppermute | solution.py:18
  72.1 0.8 fusion.35
  73.0 0.1 copy.26
  73.1 4.1 collective-permute-done.5
  77.2 9.6 %collective-permute-start.6 = (bf16[128,2048]{1,0:T(8,128)(2,1)}, bf16[128,2048]{1,0:T(8,128)(2,1)}, u32[]{:S(2)}, u32[]{:S(2)}) collective-permute-start(bf16[128,2048]{1,0:T(8,128)(2,1)} %collective-permute-done.5), channel_id=1, source_target_pairs={{0,1},{1,2},{2,3},{3,4},{4,5},{5,6},{6,7},{7,8},{8,9},{9,10},{10,1... | collective-permute-start | bytes 1572872 | tf_op jit(solution)/shard_map/ppermute | solution.py:18
  86.7 1.8 while.17
  88.6 0.6 fusion.33
  89.2 0.6 reduce_sum.66
  89.8 32.6 %all-reduce = (f32[]{:T(128)}, f32[]{:T(128)}) all-reduce(f32[]{:T(128)} %fusion.33, f32[]{:T(128)} %reduce_sum.66), channel_id=1, replica_groups=mesh['groups'=2,'fsdp'=16] {'fsdp'}, use_global_device_ids=true, to_apply=%region_9.10 | all-reduce | flops 2 | bytes 16 | tf_op jit(solution)/shard_map/psum | solution.py:108
  125.0 0.7 fusion.37
  125.8 0.5 collective-permute-start.7
  126.3 1.8 fusion.4
  128.1 0.1 reshape.79
  128.2 0.1 reshape.80
  128.3 0.7 fusion.44
  129.0 3.8 collective-permute-done.13
  132.8 4.6 collective-permute-start.14
  137.4 0.2 collective-permute-done.7
  137.5 1.1 constant_dynamic-update-slice_fusion.31
  138.6 1.1 constant_dynamic-update-slice_fusion.30
  139.7 1.1 constant_dynamic-update-slice_fusion.29
  140.8 1.1 constant_dynamic-update-slice_fusion.28
  141.9 1.1 constant_dynamic-update-slice_fusion.27
  143.1 1.1 constant_dynamic-update-slice_fusion.23
  144.2 1.1 constant_dynamic-update-slice_fusion.20
  145.3 1.1 constant_dynamic-update-slice_fusion.19
  146.4 1.1 constant_dynamic-update-slice_fusion.18
  147.5 1.1 constant_dynamic-update-slice_fusion.17
  148.6 1.1 constant_dynamic-update-slice_fusion.15
  149.7 1.1 constant_dynamic-update-slice_fusion.14
  150.8 1.1 constant_dynamic-update-slice_fusion.13
  151.9 1.1 constant_dynamic-update-slice_fusion.12
  153.3 1.1 constant_dynamic-update-slice_fusion.4
  154.4 1.1 constant_dynamic-update-slice_fusion.3
  155.4 1.1 constant_dynamic-update-slice_fusion.2
  156.5 1.1 constant_dynamic-update-slice_fusion.1
  157.7 3.6 multiply_reduce_fusion.1
  161.3 0.2 multiply_convert_fusion.1
  161.6 0.5 fusion.45
  162.2 0.1 fusion.27
  162.3 0.2 fusion.28
  162.5 1.4 fusion.29
  163.8 3.4 multiply_reduce_fusion
  167.2 0.2 reduce-scatter.2.cloned.1.call-start
  167.5 12.9 %fusion.9 = f32[2048,2048]{1,0:T(8,128)} fusion(f32[384,2048]{1,0:T(8,128)} %get-tuple-element.155, f32[384,2048]{1,0:T(8,128)S(1)} %get-tuple-element.153, f32[384]{0:T(512)S(1)} %broadcast_multiply_fusion, f32[384]{0:T(512)S(1)} %add_rsqrt_fusion, bf16[384,2048]{1,0:T(8,128)(2,1)} %param.13, f32[2048]{0:T(1024)S(1)} %copy-done.7, f32[384]{0:T(512)S(1)} %add_rsqrt_fusion.1), kind=kOutput, calls=%fused_computation.16 | convolution fusion | flops 3228303360 | bytes 24654336 | tf_op jit(solution)/shard_map/dot_general | solution.py:80
  180.4 4.1 scatter_custom_fusion
  184.5 5.3 %all-to-all-start = ((bf16[16,24,2048]{2,1,0:T(8,128)(2,1)}), bf16[16,24,2048]{2,1,0:T(8,128)(2,1)S(1)}, u32[]{:S(2)}, u32[]{:S(2)}) async-start(bf16[16,24,2048]{2,1,0:T(8,128)(2,1)} %bitcast.38), calls=%async_computation | async-start | bytes 3145728 | tf_op jit(solution)/shard_map/all_to_all | solution.py:120
  189.8 54.7 %psum.31 = f32[12]{0:T(128)} all-reduce(f32[12]{0:T(128)S(1)} %get-tuple-element.143), channel_id=1, replica_groups=mesh['groups'=2,'fsdp'=16] {'fsdp'}, use_global_device_ids=true, to_apply=%region_14.15 | all-reduce | flops 12 | bytes 96 | tf_op jit(solution)/shard_map/psum | solution.py:87
  244.5 24.4 %all-reduce.3.cloned.1.call-done = f32[2048,13]{0,1:T(8,128)} async-done(((f32[2048,13]{0,1:T(8,128)}), f32[2048,13]{0,1:T(8,128)}) %all-reduce.3.cloned.1.call-update) | async-done | bytes 106512 | tf_op jit(solution)/shard_map/psum | solution.py:87
  269.0 183.6 %reduce-scatter.2.cloned.1.call-done = f32[128,2048]{1,0:T(8,128)} async-done(((f32[2048,2048]{1,0:T(8,128)}), f32[128,2048]{1,0:T(8,128)}) %reduce-scatter.2.cloned.1.call-update) | async-done | bytes 1048592 | tf_op jit(solution)/shard_map/reduce_scatter | solution.py:79
  452.6 1.1 copy.72
  453.7 1.6 copy.73
  (105 shorter events, 2.3 us)
Async XLA Ops:
  7.2 154.4 %copy-start = (bf16[2048,13]{0,1:T(8,128)(2,1)S(1)}, bf16[2048,13]{0,1:T(8,128)(2,1)}, u32[]{:S(2)}) copy-start(bf16[2048,13]{0,1:T(8,128)(2,1)} %param.22) | copy-start | bytes 159748
  7.2 146.0 %copy-start.2 = (bf16[128,2048]{1,0:T(8,128)(2,1)S(1)}, bf16[128,2048]{1,0:T(8,128)(2,1)}, u32[]{:S(2)}) copy-start(bf16[128,2048]{1,0:T(8,128)(2,1)} %param.21) | copy-start | bytes 1572868
  7.2 261.8 %all-reduce.3.cloned.1.call-start = ((), (), s32[]{:S(2)}) async-start(), calls=%async_computation.3 | async-start | bytes 262144 | tf_op jit(solution)/shard_map/psum | solution.py:87
  7.2 12.6 %collective-permute-start = (bf16[128,2048]{1,0:T(8,128)(2,1)}, bf16[128,2048]{1,0:T(8,128)(2,1)S(1)}, u32[]{:S(2)}, u32[]{:S(2)}) collective-permute-start(bf16[128,2048]{1,0:T(8,128)(2,1)} %param.21), channel_id=1, source_target_pairs={{0,1},{1,2},{2,3},{3,4},{4,5},{5,6},{6,7},{7,8},{8,9},{9,10},{10,1... | collective-permute-start | bytes 1572872 | tf_op jit(solution)/shard_map/ppermute | solution.py:18
  19.8 11.4 %collective-permute-start.1 = (bf16[128,2048]{1,0:T(8,128)(2,1)S(1)}, bf16[128,2048]{1,0:T(8,128)(2,1)S(1)}, u32[]{:S(2)}, u32[]{:S(2)}) collective-permute-start(bf16[128,2048]{1,0:T(8,128)(2,1)S(1)} %collective-permute-done), channel_id=1, source_target_pairs={{0,1},{1,2},{2,3},{3,4},{4,5},{5,6},{6,7},{7,8},{8,9},{9,10},{10,1... | collective-permute-start | bytes 1572872 | tf_op jit(solution)/shard_map/ppermute | solution.py:18
  19.8 11.5 %collective-permute-start.8 = (bf16[128,2048]{1,0:T(8,128)(2,1)}, bf16[128,2048]{1,0:T(8,128)(2,1)S(1)}, u32[]{:S(2)}, u32[]{:S(2)}) collective-permute-start(bf16[128,2048]{1,0:T(8,128)(2,1)} %param.21), channel_id=1, source_target_pairs={{0,15},{1,0},{2,1},{3,2},{4,3},{5,4},{6,5},{7,6},{8,7},{9,8},{10,9... | collective-permute-start | bytes 1572872 | tf_op jit(solution)/shard_map/ppermute | solution.py:20
  31.2 11.4 %collective-permute-start.2 = (bf16[128,2048]{1,0:T(8,128)(2,1)S(1)}, bf16[128,2048]{1,0:T(8,128)(2,1)S(1)}, u32[]{:S(2)}, u32[]{:S(2)}) collective-permute-start(bf16[128,2048]{1,0:T(8,128)(2,1)S(1)} %collective-permute-done.1), channel_id=1, source_target_pairs={{0,1},{1,2},{2,3},{3,4},{4,5},{5,6},{6,7},{7,8},{8,9},{9,10},{10,1... | collective-permute-start | bytes 1572872 | tf_op jit(solution)/shard_map/ppermute | solution.py:18
  31.3 13.1 %collective-permute-start.9 = (bf16[128,2048]{1,0:T(8,128)(2,1)S(1)}, bf16[128,2048]{1,0:T(8,128)(2,1)S(1)}, u32[]{:S(2)}, u32[]{:S(2)}) collective-permute-start(bf16[128,2048]{1,0:T(8,128)(2,1)S(1)} %collective-permute-done.8), channel_id=1, source_target_pairs={{0,15},{1,0},{2,1},{3,2},{4,3},{5,4},{6,5},{7,6},{8,7},{9,8},{10,9... | collective-permute-start | bytes 1572872 | tf_op jit(solution)/shard_map/ppermute | solution.py:20
  42.7 11.4 %collective-permute-start.3 = (bf16[128,2048]{1,0:T(8,128)(2,1)S(1)}, bf16[128,2048]{1,0:T(8,128)(2,1)S(1)}, u32[]{:S(2)}, u32[]{:S(2)}) collective-permute-start(bf16[128,2048]{1,0:T(8,128)(2,1)S(1)} %collective-permute-done.2), channel_id=1, source_target_pairs={{0,1},{1,2},{2,3},{3,4},{4,5},{5,6},{6,7},{7,8},{8,9},{9,10},{10,1... | collective-permute-start | bytes 1572872 | tf_op jit(solution)/shard_map/ppermute | solution.py:18
  44.4 13.5 %collective-permute-start.10 = (bf16[128,2048]{1,0:T(8,128)(2,1)S(1)}, bf16[128,2048]{1,0:T(8,128)(2,1)}, u32[]{:S(2)}, u32[]{:S(2)}) collective-permute-start(bf16[128,2048]{1,0:T(8,128)(2,1)S(1)} %collective-permute-done.9), channel_id=1, source_target_pairs={{0,15},{1,0},{2,1},{3,2},{4,3},{5,4},{6,5},{7,6},{8,7},{9,8},{10,9... | collective-permute-start | bytes 1572872 | tf_op jit(solution)/shard_map/ppermute | solution.py:20
  54.1 3.8 copy-start.3
  54.1 11.5 %collective-permute-start.4 = (bf16[128,2048]{1,0:T(8,128)(2,1)S(1)}, bf16[128,2048]{1,0:T(8,128)(2,1)}, u32[]{:S(2)}, u32[]{:S(2)}) collective-permute-start(bf16[128,2048]{1,0:T(8,128)(2,1)S(1)} %collective-permute-done.3), channel_id=1, source_target_pairs={{0,1},{1,2},{2,3},{3,4},{4,5},{5,6},{6,7},{7,8},{8,9},{9,10},{10,1... | collective-permute-start | bytes 1572872 | tf_op jit(solution)/shard_map/ppermute | solution.py:18
  57.9 15.2 %collective-permute-start.11 = (bf16[128,2048]{1,0:T(8,128)(2,1)}, bf16[128,2048]{1,0:T(8,128)(2,1)}, u32[]{:S(2)}, u32[]{:S(2)}) collective-permute-start(bf16[128,2048]{1,0:T(8,128)(2,1)} %collective-permute-done.10), channel_id=1, source_target_pairs={{0,15},{1,0},{2,1},{3,2},{4,3},{5,4},{6,5},{7,6},{8,7},{9,8},{10,9... | collective-permute-start | bytes 1572872 | tf_op jit(solution)/shard_map/ppermute | solution.py:20
  65.6 11.6 %collective-permute-start.5 = (bf16[128,2048]{1,0:T(8,128)(2,1)}, bf16[128,2048]{1,0:T(8,128)(2,1)}, u32[]{:S(2)}, u32[]{:S(2)}) collective-permute-start(bf16[128,2048]{1,0:T(8,128)(2,1)} %collective-permute-done.4), channel_id=1, source_target_pairs={{0,1},{1,2},{2,3},{3,4},{4,5},{5,6},{6,7},{7,8},{8,9},{9,10},{10,1... | collective-permute-start | bytes 1572872 | tf_op jit(solution)/shard_map/ppermute | solution.py:18
  73.1 52.6 %collective-permute-start.12 = (bf16[128,2048]{1,0:T(8,128)(2,1)}, bf16[128,2048]{1,0:T(8,128)(2,1)}, u32[]{:S(2)}, u32[]{:S(2)}) collective-permute-start(bf16[128,2048]{1,0:T(8,128)(2,1)} %collective-permute-done.11), channel_id=1, source_target_pairs={{0,15},{1,0},{2,1},{3,2},{4,3},{5,4},{6,5},{7,6},{8,7},{9,8},{10,9... | collective-permute-start | bytes 1572872 | tf_op jit(solution)/shard_map/ppermute | solution.py:20
  77.2 48.6 %collective-permute-start.6 = (bf16[128,2048]{1,0:T(8,128)(2,1)}, bf16[128,2048]{1,0:T(8,128)(2,1)}, u32[]{:S(2)}, u32[]{:S(2)}) collective-permute-start(bf16[128,2048]{1,0:T(8,128)(2,1)} %collective-permute-done.5), channel_id=1, source_target_pairs={{0,1},{1,2},{2,3},{3,4},{4,5},{5,6},{6,7},{7,8},{8,9},{9,10},{10,1... | collective-permute-start | bytes 1572872 | tf_op jit(solution)/shard_map/ppermute | solution.py:18
  125.7 7.0 %collective-permute-start.13 = (bf16[128,2048]{1,0:T(8,128)(2,1)}, bf16[128,2048]{1,0:T(8,128)(2,1)}, u32[]{:S(2)}, u32[]{:S(2)}) collective-permute-start(bf16[128,2048]{1,0:T(8,128)(2,1)} %collective-permute-done.12), channel_id=1, source_target_pairs={{0,15},{1,0},{2,1},{3,2},{4,3},{5,4},{6,5},{7,6},{8,7},{9,8},{10,9... | collective-permute-start | bytes 1572872 | tf_op jit(solution)/shard_map/ppermute | solution.py:20
  125.8 11.8 %collective-permute-start.7 = (bf16[128,2048]{1,0:T(8,128)(2,1)}, bf16[128,2048]{1,0:T(8,128)(2,1)}, u32[]{:S(2)}, u32[]{:S(2)}) collective-permute-start(bf16[128,2048]{1,0:T(8,128)(2,1)} %collective-permute-done.6), channel_id=1, source_target_pairs={{0,1},{1,2},{2,3},{3,4},{4,5},{5,6},{6,7},{7,8},{8,9},{9,10},{10,1... | collective-permute-start | bytes 1572872 | tf_op jit(solution)/shard_map/ppermute | solution.py:18
  128.3 24.7 %copy-start.4 = (bf16[128,2048]{1,0:T(8,128)(2,1)S(1)}, bf16[128,2048]{1,0:T(8,128)(2,1)}, u32[]{:S(2)}) copy-start(bf16[128,2048]{1,0:T(8,128)(2,1)} %copy-done.3) | copy-start | bytes 1572868
  129.0 28.6 %copy-start.1 = (bf16[384,2048]{1,0:T(8,128)(2,1)S(1)}, bf16[384,2048]{1,0:T(8,128)(2,1)}, u32[]{:S(2)}) copy-start(bf16[384,2048]{1,0:T(8,128)(2,1)} %param.13) | copy-start | bytes 4718596
  129.0 28.7 %copy-start.7 = (f32[2048]{0:T(1024)S(1)}, f32[2048]{0:T(1024)}, u32[]{:S(2)}) copy-start(f32[2048]{0:T(1024)} %param.20) | copy-start | bytes 24580
  132.8 15.8 %collective-permute-start.14 = (bf16[128,2048]{1,0:T(8,128)(2,1)}, bf16[128,2048]{1,0:T(8,128)(2,1)S(1)}, u32[]{:S(2)}, u32[]{:S(2)}) collective-permute-start(bf16[128,2048]{1,0:T(8,128)(2,1)} %collective-permute-done.13), channel_id=1, source_target_pairs={{0,15},{1,0},{2,1},{3,2},{4,3},{5,4},{6,5},{7,6},{8,7},{9,8},{10,9... | collective-permute-start | bytes 1572872 | tf_op jit(solution)/shard_map/ppermute | solution.py:20
  157.7 4.5 copy-start.5
  157.7 4.5 copy-start.6
  167.2 285.3 %reduce-scatter.2.cloned.1.call-start = ((), (), s32[]{:S(2)}) async-start(), calls=%async_computation.2 | async-start | bytes 17825792 | tf_op jit(solution)/shard_map/reduce_scatter | solution.py:79
  167.5 12.9 %copy-start.8 = (s32[384]{0:T(512)S(1)}, s32[384]{0:T(512)}, u32[]{:S(2)}) copy-start(s32[384]{0:T(512)} %param.17) | copy-start | bytes 4612
  184.5 60.0 %all-to-all-start = ((bf16[16,24,2048]{2,1,0:T(8,128)(2,1)}), bf16[16,24,2048]{2,1,0:T(8,128)(2,1)S(1)}, u32[]{:S(2)}, u32[]{:S(2)}) async-start(bf16[16,24,2048]{2,1,0:T(8,128)(2,1)} %bitcast.38), calls=%async_computation | async-start | bytes 3145728 | tf_op jit(solution)/shard_map/all_to_all | solution.py:120
Sparse Core Ops, SparseCore 0:
  167.3 101.5 all-reduce.2
  273.6 178.8 reduce-scatter.1
